TPU v7x, 256 devices: a whole 4x4x8 slice. The times are simulated.
256 devices in a mesh: seq: 32 (over x, z), mlp: 8 (over y, core).
Axes of the slice: x: 4, y: 4, z: 8, core: 2. Of those that a mesh axis runs over, the one named last changes fastest.
Arguments:
- queries: bfloat16 [1024, 2560], P(('seq', 'mlp')), may hold values from -8 to 8
- new_kv: bfloat16 [1024, 512], P(('seq', 'mlp')), may hold values from -5 to 5
- kv_cache: bfloat16 [4352, 128, 512], P(('seq', 'mlp')), may hold values from -4 to 4, as said below
- lengths: int32 [256], replicated, may hold values from 256 to 16384, as said below
- page_table: int32 [256, 128], replicated, may hold values from -1 to 4351, as said below
- residual: bfloat16 [1024, 2560], P('seq', 'mlp'), may hold values from -3 to 3
- out_weight: bfloat16 [2560, 2560], P(None, 'mlp'), may hold values from -0.125 to 0.125
- norm_gain: float32 [2560], replicated, may hold values from 0.1 to 1.9
- gate_weight: bfloat16 [2560, 3840], P(None, 'mlp'), may hold values from -0.125 to 0.125
- up_weight: bfloat16 [2560, 3840], P(None, 'mlp'), may hold values from -0.125 to 0.125
- down_weight: bfloat16 [3840, 2560], P('mlp'), may hold values from -0.09375 to 0.09375
- next_gain: float32 [2560], replicated, may hold values from 0.1 to 1.9
- qkv_weight: bfloat16 [2560, 3072], P(None, 'mlp'), may hold values from -0.125 to 0.125
Outputs:
- attended: bfloat16 [1024, 2560], P(('seq', 'mlp'))
- residual_out: bfloat16 [1024, 2560], P('seq', 'mlp')
- next_qkv: bfloat16 [1024, 3072], P('seq', 'mlp')
Inputs may be any that keep to these rules, and one draw needn't show every extreme that they name: `lengths`: lengths have a heavy tail; at least one request has exactly 16384. page_table[r, p] is a slot exactly for the pages p holding positions max(0, lengths[r] - 2047) to lengths[r] - 1, and -1 elsewhere. Slots d * 17 to d * 17 + 16 lie on device d of seq+mlp. All pages of request r lie in consecutive slots of ONE device, whose mlp index is r modulo 8; a device may hold the pages of several requests or of none. No slot holds two pages; some device of every mlp index has all 17 slots in use. `kv_cache`: unused slots hold arbitrary values.
All inputs are finite; a program needn't handle non-finite values.
Results may differ from a plain program's by a relative error of at most 0.011.
Values may be sent and summed in bfloat16 or wider, within the bound.
No kernel may reach another device: no remote copies, remote signals or barrier semaphores. Data moves between devices by JAX's collectives and lax.ppermute only.
A program may use at most 64 MiB of HBM per device.

v0:
```python
import jax
import jax.numpy as jnp
from jax import lax
from jax.sharding import PartitionSpec as P

WINDOW = 2048
NEG_FILL = -1e30


def combine_parts(first, second):
    first_max, first_sum, first_acc = first
    second_max, second_sum, second_acc = second
    peak = jnp.maximum(first_max, second_max)
    first_factor = jnp.exp(first_max - peak)
    second_factor = jnp.exp(second_max - peak)
    return (
        peak,
        first_sum * first_factor + second_sum * second_factor,
        first_acc * first_factor[..., None] + second_acc * second_factor[..., None],
    )


def rms_norm(values, gain):
    floats = values.astype(jnp.float32)
    scaled = floats * lax.rsqrt(jnp.mean(floats * floats, axis=-1, keepdims=True) + 1e-06)
    return (scaled * gain).astype(jnp.bfloat16)


def shards(
    queries,
    new_kv,
    kv_cache,
    lengths,
    page_table,
    residual,
    out_weight,
    norm_gain,
    gate_weight,
    up_weight,
    down_weight,
    next_gain,
    qkv_weight,
):
    seq_count = lax.axis_size("seq")
    mlp_count = lax.axis_size("mlp")
    seq_place = lax.axis_index("seq")
    device = seq_place * mlp_count + lax.axis_index("mlp")
    slot_count = kv_cache.shape[0]
    page_len = kv_cache.shape[1]
    head_dim = kv_cache.shape[2] // 2
    token_count = queries.shape[0]
    width = queries.shape[1]
    head_count = width // head_dim
    request_total, page_count = page_table.shape
    scale = head_dim ** (-0.5)
    local_slot = page_table - device * slot_count
    inside = (local_slot >= 0) & (local_slot < slot_count)
    target = jnp.where(inside, local_slot, slot_count).reshape(-1)
    owners = jnp.broadcast_to(
        jnp.arange(request_total, dtype=jnp.int32)[:, None], page_table.shape
    ).reshape(-1)
    page_numbers = jnp.broadcast_to(
        jnp.arange(page_count, dtype=jnp.int32)[None, :], page_table.shape
    ).reshape(-1)
    slot_request = jnp.zeros((slot_count,), jnp.int32).at[target].set(owners, mode="drop")
    slot_page = jnp.zeros((slot_count,), jnp.int32).at[target].set(page_numbers, mode="drop")
    slot_used = jnp.zeros((slot_count,), jnp.bool_).at[target].set(True, mode="drop")
    column_rows = lax.all_gather(queries, "seq", axis=0, tiled=True)
    column_queries = column_rows.reshape(seq_count, token_count, head_count, head_dim)
    slot_column = slot_request // mlp_count
    slot_queries = column_queries[slot_column]
    cache_keys = kv_cache[:, :, :head_dim]
    cache_values = kv_cache[:, :, head_dim:]
    scores = (
        jnp.einsum("sqhd,skd->sqhk", slot_queries, cache_keys, preferred_element_type=jnp.float32)
        * scale
    )
    positions = slot_page[:, None] * page_len + jnp.arange(page_len, dtype=jnp.int32)[None, :]
    slot_length = lengths[slot_request]
    offsets = jnp.arange(token_count, dtype=jnp.int32)
    valid = (
        slot_used[:, None, None]
        & (positions[:, None, :] < slot_length[:, None, None])
        & (
            positions[:, None, :]
            >= slot_length[:, None, None] + offsets[None, :, None] - (WINDOW - 1)
        )
    )
    valid = valid[:, :, None, :]
    page_max = jnp.max(jnp.where(valid, scores, NEG_FILL), axis=-1)
    weights = jnp.where(valid, jnp.exp(scores - page_max[..., None]), 0.0)
    page_sum = jnp.sum(weights, axis=-1)
    page_acc = jnp.einsum(
        "sqhk,skd->sqhd",
        weights.astype(jnp.bfloat16),
        cache_values,
        preferred_element_type=jnp.float32,
    )
    member = (slot_column[None, :] == jnp.arange(seq_count, dtype=jnp.int32)[:, None]) & slot_used[
        None, :
    ]
    request_max = jnp.max(jnp.where(member[:, :, None, None], page_max[None], NEG_FILL), axis=1)
    rescale = jnp.exp(page_max - request_max[slot_column])
    member_float = member.astype(jnp.float32)
    request_sum = jnp.einsum(
        "rs,sqh->rqh", member_float, rescale * page_sum, precision=lax.Precision.HIGHEST
    )
    request_acc = jnp.einsum(
        "rs,sqhd->rqhd",
        member_float,
        rescale[..., None] * page_acc,
        precision=lax.Precision.HIGHEST,
    )
    got_max, got_sum, got_acc = (
        lax.all_to_all(request_max, "seq", split_axis=0, concat_axis=0, tiled=True),
        lax.all_to_all(request_sum, "seq", split_axis=0, concat_axis=0, tiled=True),
        lax.all_to_all(request_acc, "seq", split_axis=0, concat_axis=0, tiled=True),
    )
    peak = jnp.max(got_max, axis=0)
    factor = jnp.exp(got_max - peak[None])
    own_part = (
        peak,
        jnp.sum(factor * got_sum, axis=0),
        jnp.sum(factor[..., None] * got_acc, axis=0),
    )
    own_queries = queries.reshape(token_count, head_count, head_dim)
    new_keys = new_kv[:, :head_dim]
    new_values = new_kv[:, head_dim:]
    new_scores = (
        jnp.einsum("qhd,kd->qhk", own_queries, new_keys, preferred_element_type=jnp.float32) * scale
    )
    causal = (offsets[:, None] >= offsets[None, :])[:, None, :]
    new_max = jnp.max(jnp.where(causal, new_scores, NEG_FILL), axis=-1)
    new_weights = jnp.where(causal, jnp.exp(new_scores - new_max[..., None]), 0.0)
    new_sum = jnp.sum(new_weights, axis=-1)
    new_acc = jnp.einsum(
        "qhk,kd->qhd",
        new_weights.astype(jnp.bfloat16),
        new_values,
        preferred_element_type=jnp.float32,
    )
    final_max, final_sum, final_acc = combine_parts(own_part, (new_max, new_sum, new_acc))
    attended = (final_acc / final_sum[..., None]).reshape(token_count, width).astype(jnp.bfloat16)
    attention_out = jnp.dot(
        lax.all_gather(attended, "mlp", axis=0, tiled=True),
        out_weight,
        preferred_element_type=jnp.float32,
    )
    stream = (residual.astype(jnp.float32) + attention_out).astype(jnp.bfloat16)
    whole_stream = lax.all_gather(stream, "mlp", axis=1, tiled=True)
    normed = rms_norm(whole_stream, norm_gain)
    gate = jnp.dot(normed, gate_weight, preferred_element_type=jnp.float32)
    upward = jnp.dot(normed, up_weight, preferred_element_type=jnp.float32)
    hidden = (jax.nn.gelu(gate, approximate=True) * upward).astype(jnp.bfloat16)
    partial_down = jnp.dot(hidden, down_weight, preferred_element_type=jnp.float32)
    column_width = stream.shape[1]
    column_start = lax.axis_index("mlp") * column_width
    down_total = lax.psum(partial_down, "mlp")
    full_after = (whole_stream.astype(jnp.float32) + down_total).astype(jnp.bfloat16)
    shard_after = lax.dynamic_slice_in_dim(full_after, column_start, column_width, 1)
    normed_next = rms_norm(full_after, next_gain)
    next_qkv = jnp.dot(normed_next, qkv_weight, preferred_element_type=jnp.float32).astype(
        jnp.bfloat16
    )
    return (attended, shard_after, next_qkv)


def solution(mesh):
    return jax.shard_map(
        shards,
        mesh=mesh,
        in_specs=(
            P(("seq", "mlp"), None),
            P(("seq", "mlp"), None),
            P(("seq", "mlp"), None, None),
            P(),
            P(),
            P("seq", "mlp"),
            P(None, "mlp"),
            P(),
            P(None, "mlp"),
            P(None, "mlp"),
            P("mlp", None),
            P(),
            P(None, "mlp"),
        ),
        out_specs=(P(("seq", "mlp"), None), P("seq", "mlp"), P("seq", "mlp")),
        check_vma=False,
    )
```

profile of v0, /device:TPU:2, one launch (start us, length us, event | category | flops | bytes accessed | tf_op | source)
XLA Modules:
  0.0 617.3 jit_solution(3208878940347870312)
XLA Ops:
  7.2 1.1 and_select_fusion
  8.3 0.1 compare_select_fusion
  8.5 120.0 %scatter_custom_fusion = s32[17]{0:T(128)S(1)} fusion(s32[32768]{0:T(1024)S(1)} %bitcast.70, s32[32768]{0:T(1024)S(1)} %iota_bitcast_fusion.1, s32[]{:T(128)} %constant.28.clone.1), kind=kCustom, calls=%fused_computation.111 | custom fusion | bytes 72 | tf_op jit(solution)/shard_map/scatter | solution.py:65
  128.5 1.4 gather_fusion
  129.9 0.1 add_add_fusion
  130.0 120.0 %scatter_custom_fusion.2 = s32[17]{0:T(128)S(1)} fusion(s32[32768]{0:T(1024)S(1)} %bitcast.71, s32[32768]{0:T(1024)S(1)} %iota_bitcast_fusion, s32[]{:T(128)} %constant.28.clone.1), kind=kCustom, calls=%fused_computation.109 | custom fusion | bytes 72 | tf_op jit(solution)/shard_map/scatter | solution.py:66
  250.1 136.5 %scatter_custom_fusion.1 = pred[17]{0:T(512)(128)(4,1)S(1)} fusion(s32[32768]{0:T(1024)S(1)} %bitcast.72, pred[32768]{0:T(1024)(128)(4,1)S(1)} %broadcast.184, pred[]{:T(512)} %constant.20.clone.1), kind=kCustom, calls=%fused_computation.104 | custom fusion | bytes 18 | tf_op jit(solution)/shard_map/scatter | solution.py:67
  386.6 0.1 compare_and_fusion.1
  386.7 52.5 %all-gather = bf16[32,4,2560]{2,1,0:T(4,128)(2,1)S(1)} all-gather(bf16[1,4,2560]{2,1,0:T(4,128)(2,1)} %bitcast.74), channel_id=1, replica_groups=mesh['seq'=32,'mlp'=8] {'seq'}, dimensions={0}, use_global_device_ids=true | all-gather | bytes 675840 | tf_op jit(solution)/shard_map/all_gather | solution.py:68
  439.2 0.1 copy.49
  439.3 1.4 reshape.237
  440.7 2.7 gather_fusion.1
  443.3 0.1 compare_and_fusion
  443.4 2.0 select_reduce_fusion
  445.5 0.2 copy.50
  445.7 0.4 fusion.13
  446.1 0.1 fusion.43
  446.2 0.3 select_reduce_fusion.1
  446.5 0.7 copy.51
  447.2 1.4 gather_fusion.2
  448.6 0.2 fusion.37
  448.9 0.7 copy.58
  449.6 6.7 %all-to-all-start.2 = ((f32[32,4,10]{2,1,0:T(4,128)}), f32[32,4,10]{2,1,0:T(4,128)S(1)}, u32[]{:S(2)}, u32[]{:S(2)}) async-start(f32[32,4,10]{2,1,0:T(4,128)} %copy.58), calls=%async_computation.2 | async-start | bytes 131072 | tf_op jit(solution)/shard_map/all_to_all | solution.py:116
  456.3 2.7 convolution_multiply_fusion
  459.0 6.5 %all-to-all-done.2 = f32[32,4,10]{2,1,0:T(4,128)S(1)} async-done(((f32[32,4,10]{2,1,0:T(4,128)}), f32[32,4,10]{2,1,0:T(4,128)S(1)}, u32[]{:S(2)}, u32[]{:S(2)}) %all-to-all-start.2) | async-done | bytes 5152 | tf_op jit(solution)/shard_map/all_to_all | solution.py:116
  465.4 5.0 all-to-all-start
  470.4 2.3 fusion.11
  472.7 1.9 copy.55
  474.6 4.9 all-to-all-done
  479.6 6.7 %all-to-all-start.1 = ((f32[32,4,10,256]{3,1,2,0:T(4,128)}), f32[32,4,10,256]{3,1,2,0:T(4,128)}, u32[]{:S(2)}, u32[]{:S(2)}) async-start(f32[32,4,10,256]{3,1,2,0:T(4,128)} %copy.55), calls=%async_computation.1 | async-start | bytes 2621440 | tf_op jit(solution)/shard_map/all_to_all | solution.py:117
  486.4 0.2 select_reduce_fusion.2
  486.5 0.1 fusion.46
  486.7 0.3 copy.52
  487.1 18.4 %all-to-all-done.1 = f32[32,4,10,256]{3,1,2,0:T(4,128)} async-done(((f32[32,4,10,256]{3,1,2,0:T(4,128)}), f32[32,4,10,256]{3,1,2,0:T(4,128)}, u32[]{:S(2)}, u32[]{:S(2)}) %all-to-all-start.1) | async-done | bytes 1310752 | tf_op jit(solution)/shard_map/all_to_all | solution.py:117
  505.4 1.7 multiply_reduce_fusion
  507.1 0.3 fusion.3
  507.4 13.3 %all-gather.1 = bf16[8,4,2560]{2,1,0:T(4,128)(2,1)S(1)} all-gather(bf16[1,4,2560]{2,1,0:T(4,128)(2,1)S(1)} %reshape.292), channel_id=1, replica_groups=mesh['seq'=32,'mlp'=8] {'mlp'}, dimensions={0}, use_global_device_ids=true | all-gather | bytes 184320 | tf_op jit(solution)/shard_map/all_gather | solution.py:145
  520.8 2.0 fusion.10
  522.8 12.8 %all-gather.2 = bf16[8,320,32]{1,2,0:T(8,128)(2,1)S(1)} all-gather(bf16[1,320,32]{1,2,0:T(8,128)(2,1)S(1)} %fusion.10), channel_id=1, replica_groups=mesh['seq'=32,'mlp'=8] {'mlp'}, dimensions={0}, use_global_device_ids=true | all-gather | bytes 184320 | tf_op jit(solution)/shard_map/all_gather | solution.py:150
  535.7 0.1 reshape.298
  535.8 0.1 fusion.18
  536.0 2.5 fusion.74
  538.5 3.8 fusion.9
  542.3 0.6 copy.63
  542.9 63.1 %all-reduce.2.cloned.1.call-done = f32[32,2560]{1,0:T(8,128)} async-done(((f32[32,2560]{1,0:T(8,128)}), f32[32,2560]{1,0:T(8,128)}) %all-reduce.2.cloned.1.call-update) | async-done | bytes 327696 | tf_op jit(solution)/shard_map/psum | solution.py:158
  606.0 1.1 fusion.15
  607.1 0.7 constant_dynamic-slice_fusion
  607.9 2.6 convolution_convert_fusion
  (33 shorter events, 0.6 us)
Async XLA Ops:
  7.2 531.3 %copy-start = (bf16[480,2560]{1,0:T(8,128)(2,1)S(1)}, bf16[480,2560]{1,0:T(8,128)(2,1)}, u32[]{:S(2)}) copy-start(bf16[480,2560]{1,0:T(8,128)(2,1)} %param.23) | copy-start | bytes 7372804
  449.6 15.8 %all-to-all-start.2 = ((f32[32,4,10]{2,1,0:T(4,128)}), f32[32,4,10]{2,1,0:T(4,128)S(1)}, u32[]{:S(2)}, u32[]{:S(2)}) async-start(f32[32,4,10]{2,1,0:T(4,128)} %copy.58), calls=%async_computation.2 | async-start | bytes 131072 | tf_op jit(solution)/shard_map/all_to_all | solution.py:116
  465.4 14.2 %all-to-all-start = ((f32[32,4,10]{2,1,0:T(4,128)}), f32[32,4,10]{2,1,0:T(4,128)S(1)}, u32[]{:S(2)}, u32[]{:S(2)}) async-start(f32[32,4,10]{2,1,0:T(4,128)} %copy.51), calls=%async_computation | async-start | bytes 131072 | tf_op jit(solution)/shard_map/all_to_all | solution.py:115
  474.6 11.7 %copy-start.1 = (bf16[4,2560]{1,0:T(4,128)(2,1)S(1)}, bf16[4,2560]{1,0:T(4,128)(2,1)}, u32[]{:S(2)}) copy-start(bf16[4,2560]{1,0:T(4,128)(2,1)} %param.13) | copy-start | bytes 61444
  474.6 11.7 %copy-start.5 = (bf16[4,512]{1,0:T(4,128)(2,1)S(1)}, bf16[4,512]{1,0:T(4,128)(2,1)}, u32[]{:S(2)}) copy-start(bf16[4,512]{1,0:T(4,128)(2,1)} %param.14) | copy-start | bytes 12292
  479.6 25.8 %all-to-all-start.1 = ((f32[32,4,10,256]{3,1,2,0:T(4,128)}), f32[32,4,10,256]{3,1,2,0:T(4,128)}, u32[]{:S(2)}, u32[]{:S(2)}) async-start(f32[32,4,10,256]{3,1,2,0:T(4,128)} %copy.55), calls=%async_computation.1 | async-start | bytes 2621440 | tf_op jit(solution)/shard_map/all_to_all | solution.py:117
  486.3 34.5 %copy-start.3 = (bf16[32,320]{1,0:T(8,128)(2,1)S(1)}, bf16[32,320]{1,0:T(8,128)(2,1)}, u32[]{:S(2)}) copy-start(bf16[32,320]{1,0:T(8,128)(2,1)} %param.18) | copy-start | bytes 61444
  486.3 119.8 %all-reduce.2.cloned.1.call-start = ((), (), s32[]{:S(2)}) async-start(), calls=%async_computation.3 | async-start | bytes 655360 | tf_op jit(solution)/shard_map/psum | solution.py:158
  520.7 15.2 %copy-start.2 = (f32[2560]{0:T(1024)S(1)}, f32[2560]{0:T(1024)}, u32[]{:S(2)}) copy-start(f32[2560]{0:T(1024)} %param.20) | copy-start | bytes 30724
  538.4 69.4 %copy-start.4 = (f32[2560]{0:T(1024)S(1)}, f32[2560]{0:T(1024)}, u32[]{:S(2)}) copy-start(f32[2560]{0:T(1024)} %param.24) | copy-start | bytes 30724
Sparse Core Ops, SparseCore 0:
  542.4 63.6 all-reduce.1
where the time goes:
time: 618 us; the launch traced here: 617 us
  local copies, waits for them, and re-layouts  389 us (63%)
  waiting for transfers between devices  92.9 us (15%)
  blocking collectives  78.6 us (13%)
  matrix products  18.6 us (3%)
  starting transfers between devices  18.3 us (3%)
  between operations  14.3 us (2%)
    scatter x1, local copies, waits for them, and re-layouts, shards(): jnp.zeros((slot_count,), jnp.bool_).at[target].set(True, mode='drop')  136 us
    scatter x1, local copies, waits for them, and re-layouts, shards(): jnp.zeros((slot_count,), jnp.int32).at[target].set(owners, mode='drop')  120 us
    scatter x1, local copies, waits for them, and re-layouts, shards(): jnp.zeros((slot_count,), jnp.int32).at[target]  120 us
    psum x1, waiting for transfers between devices, shards(): down_total = lax.psum(partial_down, 'mlp')  63.1 us
    all_gather x1, blocking collectives, shards(): column_rows = lax.all_gather(queries, 'seq', axis=0, tiled=True)  52.5 us
    all_to_all x1, waiting for transfers between devices, shards(): lax.all_to_all(request_acc, 'seq', split_axis=0, concat_axis=0, tiled=True)  18.4 us
    all_gather x1, blocking collectives, shards(): lax.all_gather(attended, 'mlp', axis=0, tiled=True)  13.3 us
    all_gather x1, blocking collectives, shards(): whole_stream = lax.all_gather(stream, 'mlp', axis=1, tiled=True)  12.8 us
  transfers between devices with their start and end apart: 4, of which 4 were waited for; matrix products, arithmetic and copies ran while one was open for 1% of the time, Pallas kernels for 0%

commit v1 on v0

--- a/solution.py
+++ b/solution.py
@@ -41,6 +41,11 @@
     next_gain,
     qkv_weight,
 ):
+
+    def proceed_pairs_all_now(vector, lane_axis):
+        x_new = lax.all_gather(vector, axis_name=lane_axis).sum(axis=0)
+        return x_new
+
     seq_count = lax.axis_size("seq")
     mlp_count = lax.axis_size("mlp")
     seq_place = lax.axis_index("seq")
@@ -155,7 +160,7 @@
     partial_down = jnp.dot(hidden, down_weight, preferred_element_type=jnp.float32)
     column_width = stream.shape[1]
     column_start = lax.axis_index("mlp") * column_width
-    down_total = lax.psum(partial_down, "mlp")
+    down_total = proceed_pairs_all_now(partial_down, lane_axis="mlp")
     full_after = (whole_stream.astype(jnp.float32) + down_total).astype(jnp.bfloat16)
     shard_after = lax.dynamic_slice_in_dim(full_after, column_start, column_width, 1)
     normed_next = rms_norm(full_after, next_gain)

time: 618 us -> 582 us (0.942)
  waiting for transfers between devices: 92.9 us -> 53.8 us
    psum x1 -> x0, waiting for transfers between devices: 63.1 us -> none  [shards(): down_total = lax.psum(partial_down, 'mlp')]
    all_gather x0 -> x1, waiting for transfers between devices: none -> 26.2 us  [proceed_pairs_all_now(): x_new = lax.all_gather(vector, axis_name=lane_axis).sum(axis=0)]
  transfers between devices with their start and end apart: 4 -> 4, of which waited for: 4 -> 4; matrix products, arithmetic and copies ran while one was open for 1% -> 2% of each run, Pallas kernels for 0% -> 0%
where the time goes in v1:
time: 582 us; the launch traced here: 580 us
  local copies, waits for them, and re-layouts  389 us (67%)
  blocking collectives  78.6 us (14%)
  waiting for transfers between devices  53.8 us (9%)
  starting transfers between devices  19 us (3%)
  matrix products  18.6 us (3%)
  between operations  14.3 us (2%)
  other arithmetic  6.5 us (1%)
    scatter x1, local copies, waits for them, and re-layouts, shards(): jnp.zeros((slot_count,), jnp.bool_).at[target].set(True, mode='drop')  136 us
    scatter x1, local copies, waits for them, and re-layouts, shards(): jnp.zeros((slot_count,), jnp.int32).at[target].set(owners, mode='drop')  120 us
    scatter x1, local copies, waits for them, and re-layouts, shards(): jnp.zeros((slot_count,), jnp.int32).at[target]  120 us
    all_gather x1, blocking collectives, shards(): column_rows = lax.all_gather(queries, 'seq', axis=0, tiled=True)  52.5 us
    all_gather x1, waiting for transfers between devices, proceed_pairs_all_now(): x_new = lax.all_gather(vector, axis_name=lane_axis).sum(axis=0)  26.2 us
    all_to_all x1, waiting for transfers between devices, shards(): lax.all_to_all(request_acc, 'seq', split_axis=0, concat_axis=0, tiled=True)  18.7 us
    all_gather x1, blocking collectives, shards(): lax.all_gather(attended, 'mlp', axis=0, tiled=True)  13.3 us
    all_gather x1, blocking collectives, shards(): whole_stream = lax.all_gather(stream, 'mlp', axis=1, tiled=True)  12.8 us
  transfers between devices with their start and end apart: 4, of which 4 were waited for; matrix products, arithmetic and copies ran while one was open for 2% of the time, Pallas kernels for 0%

profile of v1, /device:TPU:2, one launch (start us, length us, event | category | flops | bytes accessed | tf_op | source)
XLA Modules:
  0.0 579.8 jit_solution(6181970287313349444)
XLA Ops:
  7.2 1.1 and_select_fusion
  8.3 0.1 compare_select_fusion
  8.5 120.0 %scatter_custom_fusion = s32[17]{0:T(128)S(1)} fusion(s32[32768]{0:T(1024)S(1)} %bitcast.75, s32[32768]{0:T(1024)S(1)} %iota_bitcast_fusion.1, s32[]{:T(128)} %constant.28.clone.1), kind=kCustom, calls=%fused_computation.111 | custom fusion | bytes 72 | tf_op jit(solution)/shard_map/scatter | solution.py:70
  128.5 1.4 gather_fusion
  130.0 120.0 %scatter_custom_fusion.2 = s32[17]{0:T(128)S(1)} fusion(s32[32768]{0:T(1024)S(1)} %bitcast.76, s32[32768]{0:T(1024)S(1)} %iota_bitcast_fusion, s32[]{:T(128)} %constant.28.clone.1), kind=kCustom, calls=%fused_computation.109 | custom fusion | bytes 72 | tf_op jit(solution)/shard_map/scatter | solution.py:71
  250.1 136.5 %scatter_custom_fusion.1 = pred[17]{0:T(512)(128)(4,1)S(1)} fusion(s32[32768]{0:T(1024)S(1)} %bitcast.77, pred[32768]{0:T(1024)(128)(4,1)S(1)} %broadcast.184, pred[]{:T(512)} %constant.20.clone.1), kind=kCustom, calls=%fused_computation.104 | custom fusion | bytes 18 | tf_op jit(solution)/shard_map/scatter | solution.py:72
  386.6 0.1 compare_and_fusion.1
  386.7 0.1 fusion.43
  386.8 52.5 %all-gather.1 = bf16[32,4,2560]{2,1,0:T(4,128)(2,1)S(1)} all-gather(bf16[1,4,2560]{2,1,0:T(4,128)(2,1)} %bitcast.79), channel_id=1, replica_groups=mesh['seq'=32,'mlp'=8] {'seq'}, dimensions={0}, use_global_device_ids=true | all-gather | bytes 675840 | tf_op jit(solution)/shard_map/all_gather | solution.py:73
  439.3 0.1 copy.49
  439.4 1.4 reshape.237
  440.8 2.7 gather_fusion.1
  443.4 0.1 compare_and_fusion
  443.5 2.0 select_reduce_fusion
  445.6 0.2 copy.50
  445.8 0.3 select_reduce_fusion.1
  446.0 0.7 copy.51
  446.8 6.7 %all-to-all-start = ((f32[32,4,10]{2,1,0:T(4,128)}), f32[32,4,10]{2,1,0:T(4,128)S(1)}, u32[]{:S(2)}, u32[]{:S(2)}) async-start(f32[32,4,10]{2,1,0:T(4,128)} %copy.51), calls=%async_computation | async-start | bytes 131072 | tf_op jit(solution)/shard_map/all_to_all | solution.py:120
  453.4 1.5 gather_fusion.2
  454.9 0.4 fusion.13
  455.4 2.7 convolution_multiply_fusion
  458.0 0.2 fusion.37
  458.3 0.7 copy.58
  459.0 3.3 all-to-all-done
  462.3 6.5 %all-to-all-start.2 = ((f32[32,4,10]{2,1,0:T(4,128)}), f32[32,4,10]{2,1,0:T(4,128)S(1)}, u32[]{:S(2)}, u32[]{:S(2)}) async-start(f32[32,4,10]{2,1,0:T(4,128)} %copy.58), calls=%async_computation.2 | async-start | bytes 131072 | tf_op jit(solution)/shard_map/all_to_all | solution.py:121
  468.8 2.3 fusion.11
  471.2 1.9 copy.55
  473.1 5.6 all-to-all-done.2
  478.7 5.7 all-to-all-start.1
  484.5 0.2 select_reduce_fusion.2
  484.7 0.1 fusion.46
  484.9 0.3 copy.52
  485.2 18.7 %all-to-all-done.1 = f32[32,4,10,256]{3,1,2,0:T(4,128)} async-done(((f32[32,4,10,256]{3,1,2,0:T(4,128)}), f32[32,4,10,256]{3,1,2,0:T(4,128)}, u32[]{:S(2)}, u32[]{:S(2)}) %all-to-all-start.1) | async-done | bytes 1310752 | tf_op jit(solution)/shard_map/all_to_all | solution.py:122
  503.9 1.7 multiply_reduce_fusion
  505.7 0.3 fusion.3
  506.0 13.3 %all-gather.2 = bf16[8,4,2560]{2,1,0:T(4,128)(2,1)S(1)} all-gather(bf16[1,4,2560]{2,1,0:T(4,128)(2,1)S(1)} %reshape.293), channel_id=1, replica_groups=mesh['seq'=32,'mlp'=8] {'mlp'}, dimensions={0}, use_global_device_ids=true | all-gather | bytes 184320 | tf_op jit(solution)/shard_map/all_gather | solution.py:150
  519.3 2.0 fusion.10
  521.4 12.8 %all-gather.3 = bf16[8,320,32]{1,2,0:T(8,128)(2,1)S(1)} all-gather(bf16[1,320,32]{1,2,0:T(8,128)(2,1)S(1)} %fusion.10), channel_id=1, replica_groups=mesh['seq'=32,'mlp'=8] {'mlp'}, dimensions={0}, use_global_device_ids=true | all-gather | bytes 184320 | tf_op jit(solution)/shard_map/all_gather | solution.py:155
  534.2 0.1 reshape.299
  534.3 0.1 fusion.18
  534.5 2.5 fusion.74
  537.0 3.8 fusion.9
  540.8 0.6 copy.63
  541.4 26.2 %all-gather.6.cloned.1.call-done = f32[256,2560]{1,0:T(8,128)} async-done(((f32[32,2560]{1,0:T(8,128)}), f32[256,2560]{1,0:T(8,128)}) %all-gather.6.cloned.1.call-update) | async-done | bytes 2621456 | tf_op jit(solution)/shard_map/all_gather | solution.py:46
  567.6 1.9 reduce_sum.68
  569.5 0.2 fusion.15
  569.7 0.7 constant_dynamic-slice_fusion
  570.4 2.6 convolution_convert_fusion
  (34 shorter events, 0.6 us)
Async XLA Ops:
  7.2 529.8 %copy-start = (bf16[480,2560]{1,0:T(8,128)(2,1)S(1)}, bf16[480,2560]{1,0:T(8,128)(2,1)}, u32[]{:S(2)}) copy-start(bf16[480,2560]{1,0:T(8,128)(2,1)} %param.23) | copy-start | bytes 7372804
  446.8 15.5 %all-to-all-start = ((f32[32,4,10]{2,1,0:T(4,128)}), f32[32,4,10]{2,1,0:T(4,128)S(1)}, u32[]{:S(2)}, u32[]{:S(2)}) async-start(f32[32,4,10]{2,1,0:T(4,128)} %copy.51), calls=%async_computation | async-start | bytes 131072 | tf_op jit(solution)/shard_map/all_to_all | solution.py:120
  462.3 16.4 %all-to-all-start.2 = ((f32[32,4,10]{2,1,0:T(4,128)}), f32[32,4,10]{2,1,0:T(4,128)S(1)}, u32[]{:S(2)}, u32[]{:S(2)}) async-start(f32[32,4,10]{2,1,0:T(4,128)} %copy.58), calls=%async_computation.2 | async-start | bytes 131072 | tf_op jit(solution)/shard_map/all_to_all | solution.py:121
  473.1 11.4 %copy-start.1 = (bf16[4,2560]{1,0:T(4,128)(2,1)S(1)}, bf16[4,2560]{1,0:T(4,128)(2,1)}, u32[]{:S(2)}) copy-start(bf16[4,2560]{1,0:T(4,128)(2,1)} %param.13) | copy-start | bytes 61444
  473.1 11.4 %copy-start.5 = (bf16[4,512]{1,0:T(4,128)(2,1)S(1)}, bf16[4,512]{1,0:T(4,128)(2,1)}, u32[]{:S(2)}) copy-start(bf16[4,512]{1,0:T(4,128)(2,1)} %param.14) | copy-start | bytes 12292
  478.7 25.3 %all-to-all-start.1 = ((f32[32,4,10,256]{3,1,2,0:T(4,128)}), f32[32,4,10,256]{3,1,2,0:T(4,128)}, u32[]{:S(2)}, u32[]{:S(2)}) async-start(f32[32,4,10,256]{3,1,2,0:T(4,128)} %copy.55), calls=%async_computation.1 | async-start | bytes 2621440 | tf_op jit(solution)/shard_map/all_to_all | solution.py:122
  484.4 34.9 %copy-start.3 = (bf16[32,320]{1,0:T(8,128)(2,1)S(1)}, bf16[32,320]{1,0:T(8,128)(2,1)}, u32[]{:S(2)}) copy-start(bf16[32,320]{1,0:T(8,128)(2,1)} %param.18) | copy-start | bytes 61444
  484.4 83.2 %all-gather.6.cloned.1.call-start = ((), (), s32[]{:S(2)}) async-start(), calls=%async_computation.3 | async-start | bytes 2949120 | tf_op jit(solution)/shard_map/all_gather | solution.py:46
  519.3 15.2 %copy-start.2 = (f32[2560]{0:T(1024)S(1)}, f32[2560]{0:T(1024)}, u32[]{:S(2)}) copy-start(f32[2560]{0:T(1024)} %param.20) | copy-start | bytes 30724
  540.8 29.6 %copy-start.4 = (f32[2560]{0:T(1024)S(1)}, f32[2560]{0:T(1024)}, u32[]{:S(2)}) copy-start(f32[2560]{0:T(1024)} %param.24) | copy-start | bytes 30724
Sparse Core Ops, SparseCore 0:
  540.9 26.6 all-gather.5
